TPU v7x, 512 devices: a whole 4x8x8 slice. The times are simulated.
512 devices in a mesh: dp: 4 (over x), expert: 8 (over y), etp: 16 (over z, core).
Axes of the slice: x: 4, y: 8, z: 8, core: 2. Of those that a mesh axis runs over, the one named last changes fastest.
Arguments:
- tokens: bfloat16 [4096, 3072], P(('dp', 'expert')), parts along dimension 0, may hold values from -6 to 6
- routes: int32 [4096, 2], P(('dp', 'expert')), parts along dimension 0, may hold values from 0 to 3, all different within a row; in each aligned block of 128 rows (0 to 127, 128 to 255, ...) at most 80 rows name the same one
- route_weight: float32 [4096, 2], P(('dp', 'expert')), parts along dimension 0, may hold values from 0.2 to 1
- w_in: bfloat16 [8, 3072, 4096], P('expert', None, 'etp'), may hold values from -0.109375 to 0.109375
- w_out: bfloat16 [8, 4096, 3072], P('expert', 'etp'), may hold values from -0.0625 to 0.0625
Outputs:
- moe_output: bfloat16 [4096, 3072], P(('dp', 'expert')), parts along dimension 0
There are 4 independent parts, one for each index of `dp`. A program takes and returns all parts, laid end to end along the dimension named above; an argument that names none is the same for every part. Nothing has to cross between parts.
Inputs may be any that keep to these rules, and one draw needn't show every extreme that they name: `routes`: each row names two different experts. Within each aligned block of 128 rows (the rows of one index of the expert axis) no expert is named by more than 80 rows, a bound that some block reaches.
All inputs are finite; a program needn't handle non-finite values.
Results may differ from a plain program's by a relative error of at most 0.018.
Values may be sent and summed in bfloat16 or wider, within the bound.
No kernel may reach another device: no remote copies, remote signals or barrier semaphores. Data moves between devices by JAX's collectives and lax.ppermute only.
A program may use at most 64 MiB of HBM per device.

v0:
```python
import jax
import jax.numpy as jnp
from jax import lax
from jax.sharding import PartitionSpec as P


def on_device(tokens, routes, route_weight, w_in, w_out):
    n_index = lax.axis_size("expert")
    n_tensor = lax.axis_size("etp")
    halves = max(1, n_index // 4)
    n_experts = n_index // halves
    tok_rows = tokens.shape[0]
    model_width = tokens.shape[1]
    rounded_up = (2 * tok_rows // n_experts + tok_rows // 8 + n_tensor - 1) // n_tensor * n_tensor
    capacity = min(tok_rows, rounded_up)
    chosen = routes.reshape(-1)
    indicator = (chosen[:, None] == jnp.arange(n_experts, dtype=jnp.int32)[None, :]).astype(
        jnp.int32
    )
    preceding = jnp.cumsum(indicator, axis=0) - indicator
    position = jnp.sum(preceding * indicator, axis=1)
    destination = chosen * capacity + position
    duplicated = jnp.repeat(tokens, 2, axis=0)
    packed = (
        jnp.zeros((n_experts * capacity, model_width), jnp.bfloat16).at[destination].set(duplicated)
    )
    outgoing = jnp.repeat(packed.reshape(n_experts, capacity, model_width), halves, axis=0)
    w_first = w_in[0]
    w_second = w_out[0]
    arrived = lax.all_to_all(outgoing, "expert", split_axis=0, concat_axis=0, tiled=True)
    flat_rows = arrived.reshape(-1, model_width)
    projected = jnp.dot(flat_rows, w_first, preferred_element_type=jnp.float32)
    hidden = jax.nn.silu(projected).astype(jnp.bfloat16)
    term = jnp.dot(hidden, w_second, preferred_element_type=jnp.float32)
    rounded = lax.optimization_barrier(term.astype(jnp.bfloat16))
    partial_terms = rounded.astype(jnp.float32).reshape(arrived.shape[:-1] + (model_width,))
    summed = lax.psum_scatter(
        partial_terms.astype(jnp.bfloat16), "etp", scatter_dimension=1, tiled=True
    ).astype(jnp.float32)
    homeward = lax.all_to_all(
        summed.astype(jnp.bfloat16), "expert", split_axis=0, concat_axis=0, tiled=True
    ).astype(summed.dtype)
    gathered = lax.all_gather(homeward.astype(jnp.bfloat16), "etp", axis=1, tiled=True).astype(
        homeward.dtype
    )
    home_rows = gathered.reshape(n_index * capacity, model_width)
    combined = jnp.zeros((tok_rows * 2, model_width), jnp.float32)
    for half_index in range(halves):
        combined = combined + home_rows[(chosen * halves + half_index) * capacity + position]
    weighted = combined.reshape(tok_rows, 2, model_width) * route_weight[:, :, None]
    return jnp.sum(weighted, axis=1).astype(jnp.bfloat16)


def solution(mesh):
    placed = (
        P(("dp", "expert"), None),
        P(("dp", "expert"), None),
        P(("dp", "expert"), None),
        P("expert", None, "etp"),
        P("expert", "etp", None),
    )
    return jax.shard_map(
        on_device, mesh=mesh, in_specs=placed, out_specs=P(("dp", "expert"), None), check_vma=False
    )
```

profile of v0, /device:TPU:1, one launch (start us, length us, event | category | flops | bytes accessed | tf_op | source)
XLA Modules:
  0.0 307.0 jit_solution(10249326293521199883)
XLA Ops:
  6.5 0.9 copy.28
  7.7 0.7 add_multiply_fusion
  8.4 1.2 reduce-window.6
  10.1 0.1 mul.69
  10.4 0.1 mul.74
  10.7 0.1 mul.77
  10.8 1.9 broadcast_in_dim.7
  12.8 1.5 reshape.166
  14.3 4.2 %scatter_custom_fusion = bf16[320,3072]{1,0:T(8,128)(2,1)S(1)} fusion(s32[256]{0:T(256)S(1)} %bitcast.49, bf16[256,3072]{1,0:T(8,128)(2,1)} %reshape.166, bf16[]{:T(256)} %constant.5.clone.1), kind=kCustom, calls=%fused_computation.8 | custom fusion | bytes 1966592 | tf_op jit(solution)/shard_map/scatter | solution.py:25
  18.5 0.6 broadcast_in_dim.16
  19.1 95.2 %all_to_all.10 = bf16[8,80,3072]{2,1,0:T(8,128)(2,1)} all-to-all(bf16[8,80,3072]{2,1,0:T(8,128)(2,1)S(1)} %bitcast.41), channel_id=1, replica_groups=mesh['dp'=4,'expert'=8,'etp'=16] {'expert'}, dimensions={0} | all-to-all | bytes 7864320 | tf_op jit(solution)/shard_map/all_to_all | solution.py:30
  114.4 8.2 %convolution_convert_fusion = bf16[640,3072]{1,0:T(8,128)(2,1)} fusion(bf16[1,256,3072]{2,1,0:T(8,128)(2,1)S(1)} %copy-done, bf16[640,3072]{1,0:T(8,128)(2,1)} %bitcast.43, bf16[1,3072,256]{2,1,0:T(8,128)(2,1)S(1)} %copy-done.2), kind=kOutput, calls=%fused_computation.3 | convolution fusion | flops 2016051200 | bytes 11010048 | tf_op jit(solution)/shard_map/dot_general | solution.py:34
  122.5 6.2 %copy.32 = bf16[8,80,3072]{2,0,1:T(8,128)(2,1)} copy(bf16[8,80,3072]{2,1,0:T(8,128)(2,1)} %bitcast.44) | data formatting | bytes 7864320 | tf_op jit(solution)/shard_map/convert_element_type | solution.py:38
  128.8 66.1 %reduce-scatter.2.cloned.1.call-done = bf16[8,5,3072]{2,0,1:T(8,128)(2,1)} async-done(((bf16[8,80,3072]{2,0,1:T(8,128)(2,1)}), bf16[8,5,3072]{2,0,1:T(8,128)(2,1)}) %reduce-scatter.2.cloned.1.call-update) | async-done | bytes 245776 | tf_op jit(solution)/shard_map/reduce_scatter | solution.py:37
  194.9 1.1 copy.33
  196.0 16.7 %all_to_all.11 = bf16[8,5,3072]{2,1,0:T(8,128)(2,1)S(1)} all-to-all(bf16[8,5,3072]{2,1,0:T(8,128)(2,1)S(1)} %copy.33), channel_id=1, replica_groups=mesh['dp'=4,'expert'=8,'etp'=16] {'expert'}, dimensions={0} | all-to-all | bytes 491520 | tf_op jit(solution)/shard_map/all_to_all | solution.py:40
  212.8 0.9 copy.34
  213.8 45.4 %all-gather.2.cloned.1.call-done = bf16[8,80,3072]{2,0,1:T(8,128)(2,1)} async-done(((bf16[8,5,3072]{2,0,1:T(8,128)(2,1)}), bf16[8,80,3072]{2,0,1:T(8,128)(2,1)}) %all-gather.2.cloned.1.call-update) | async-done | bytes 3932176 | tf_op jit(solution)/shard_map/all_gather | solution.py:43
  259.2 7.5 %copy.35 = f32[8,80,3072]{2,1,0:T(8,128)} copy(bf16[8,80,3072]{2,0,1:T(8,128)(2,1)} %all-gather.2.cloned.1.call-done) | data formatting | bytes 11796480 | tf_op jit(solution)/shard_map/reshape | solution.py:46
  266.7 8.0 %gather_fusion.1 = f32[256,3072]{1,0:T(8,128)} fusion(f32[640,3072]{1,0:T(8,128)} %bitcast.39, s32[1024]{0:T(1024)S(1)} %pad_clamp_fusion), kind=kCustom, calls=%fused_computation.1 | custom fusion | bytes 6292480 | tf_op jit(solution)/shard_map/gather | solution.py:49
  274.7 8.0 %gather_fusion = f32[256,3072]{1,0:T(8,128)} fusion(f32[640,3072]{1,0:T(8,128)} %bitcast.40, s32[1024]{0:T(1024)S(1)} %pad_clamp_fusion.1), kind=kCustom, calls=%fused_computation | custom fusion | bytes 6292480 | tf_op jit(solution)/shard_map/gather | solution.py:49
  282.7 5.1 %add.100 = f32[256,3072]{1,0:T(8,128)} add(f32[256,3072]{1,0:T(8,128)} %gather_fusion, f32[256,3072]{1,0:T(8,128)} %gather_fusion.1) | non-fusion elementwise | flops 786432 | bytes 9437184 | tf_op jit(solution)/shard_map/add | solution.py:49
  287.8 5.1 %add.101 = f32[128,2,3072]{2,1,0:T(2,128)} reshape(f32[256,3072]{1,0:T(8,128)} %add.100) | data formatting | bytes 6291456 | tf_op jit(solution)/shard_map/add | solution.py:49
  292.8 7.3 %multiply_reduce_fusion = bf16[128,3072]{1,0:T(8,128)(2,1)} fusion(f32[128,2,3072]{2,1,0:T(2,128)} %add.101, f32[128,2]{1,0:T(8,128)S(1)} %copy.38), kind=kLoop, calls=%fused_computation.4 | loop fusion | flops 1179648 | bytes 3933184 | tf_op jit(solution)/shard_map/reduce_sum | solution.py:51
  (27 shorter events, 1.3 us)
Async XLA Ops:
  6.5 107.8 %copy-start = (bf16[1,256,3072]{2,1,0:T(8,128)(2,1)S(1)}, bf16[1,256,3072]{2,1,0:T(8,128)(2,1)}, u32[]{:S(2)}) copy-start(bf16[1,256,3072]{2,1,0:T(8,128)(2,1)} %param.9) | copy-start | bytes 4718596
  6.5 188.4 %reduce-scatter.2.cloned.1.call-start = ((), (), s32[]{:S(2)}) async-start(), calls=%async_computation.3 | async-start | bytes 4177920 | tf_op jit(solution)/shard_map/reduce_scatter | solution.py:37
  19.1 95.2 %copy-start.2 = (bf16[1,3072,256]{2,1,0:T(8,128)(2,1)S(1)}, bf16[1,3072,256]{2,1,0:T(8,128)(2,1)}, u32[]{:S(2)}) copy-start(bf16[1,3072,256]{2,1,0:T(8,128)(2,1)} %param.8) | copy-start | bytes 4718596
  128.7 84.9 %copy-start.1 = (f32[128,2]{0,1:T(2,128)S(1)}, f32[128,2]{0,1:T(2,128)}, u32[]{:S(2)}) copy-start(f32[128,2]{0,1:T(2,128)} %param.7) | copy-start | bytes 3076
  128.7 130.5 %all-gather.2.cloned.1.call-start = ((), (), s32[]{:S(2)}) async-start(), calls=%async_computation.4 | async-start | bytes 4177920 | tf_op jit(solution)/shard_map/all_gather | solution.py:43
Sparse Core Ops, SparseCore 0:
  128.9 66.0 reduce-scatter.1
  213.8 45.4 all-gather.1
where the time goes:
time: 308 us; the launch traced here: 307 us
  blocking collectives  112 us (36%)
  waiting for transfers between devices  112 us (36%)
  local copies, waits for them, and re-layouts  47.3 us (15%)
  other arithmetic  14.4 us (5%)
  between operations  13.5 us (4%)
  matrix products  8.18 us (3%)
    all_to_all x1, blocking collectives, on_device(): lax.all_to_all(outgoing, 'expert', split_axis=0, concat_axis=0, tiled=True)  95.2 us
    reduce_scatter x1, waiting for transfers between devices, on_device(): lax.psum_scatter(partial_terms.astype(jnp.bfloat16), 'etp', scatter_dimen...  66.1 us
    all_gather x1, waiting for transfers between devices, on_device(): lax.all_gather(homeward.astype(jnp.bfloat16), 'etp', axis=1, tiled=True)  45.4 us
    all_to_all x1, blocking collectives, on_device(): lax.all_to_all(summed.astype(jnp.bfloat16), 'expert', split_axis=0, conca...  16.7 us
    gather x2, local copies, waits for them, and re-layouts, on_device(): home_rows[(chosen * halves + half_index) * capacity + position]  16 us
    dot_general x1, matrix products, on_device(): term = jnp.dot(hidden, w_second, preferred_element_type=jnp.float32)  8.18 us
    reshape x1, local copies, waits for them, and re-layouts, on_device(): home_rows = gathered.reshape(n_index * capacity, model_width)  7.47 us
    reduce_sum x1, other arithmetic, on_device(): return jnp.sum(weighted, axis=1).astype(jnp.bfloat16)  7.27 us
  transfers between devices with their start and end apart: 2, of which 2 were waited for; matrix products, arithmetic and copies ran while one was open for 0% of the time, Pallas kernels for 0%

commit v1 on v0

--- a/solution.py
+++ b/solution.py
@@ -40,9 +40,12 @@
     homeward = lax.all_to_all(
         summed.astype(jnp.bfloat16), "expert", split_axis=0, concat_axis=0, tiled=True
     ).astype(summed.dtype)
-    gathered = lax.all_gather(homeward.astype(jnp.bfloat16), "etp", axis=1, tiled=True).astype(
-        homeward.dtype
-    )
+    gathered = jnp.concatenate(
+        lax.all_to_all(
+            jnp.stack([homeward.astype(jnp.bfloat16)] * lax.axis_size("etp")), "etp", 0, 0
+        ),
+        axis=1,
+    ).astype(homeward.dtype)
     home_rows = gathered.reshape(n_index * capacity, model_width)
     combined = jnp.zeros((tok_rows * 2, model_width), jnp.float32)
     for half_index in range(halves):

time: 308 us -> 379 us (1.23)
  waiting for transfers between devices: 112 us -> 154 us
  local copies, waits for them, and re-layouts: 47.3 us -> 61 us
  starting transfers between devices: 0.04 us -> 11.7 us
    all_to_all x0 -> x1, waiting for transfers between devices: none -> 87.8 us  [on_device(): lax.all_to_all(jnp.stack([homeward.astype(jnp.bfloat16)] * lax.axis_size(...]
    all_gather x1 -> x0, waiting for transfers between devices: 45.4 us -> none  [on_device(): lax.all_gather(homeward.astype(jnp.bfloat16), 'etp', axis=1, tiled=True)]
    convert_element_type x0 -> x2, local copies, waits for them, and re-layouts: none -> 19.6 us  [on_device(): gathered = jnp.concatenate(lax.all_to_all(jnp.stack([homeward.astype(jnp....]
    all_to_all x0 -> x1, starting transfers between devices: none -> 11.7 us  [on_device(): lax.all_to_all(jnp.stack([homeward.astype(jnp.bfloat16)] * lax.axis_size(...]
    reshape x1 -> x0, local copies, waits for them, and re-layouts: 7.47 us -> none  [on_device(): home_rows = gathered.reshape(n_index * capacity, model_width)]
where the time goes in v1:
time: 379 us; the launch traced here: 378 us
  waiting for transfers between devices  154 us (41%)
  blocking collectives  112 us (30%)
  local copies, waits for them, and re-layouts  61 us (16%)
  other arithmetic  17.5 us (5%)
  between operations  13.5 us (4%)
  starting transfers between devices  11.7 us (3%)
  matrix products  8.18 us (2%)
    all_to_all x1, blocking collectives, on_device(): lax.all_to_all(outgoing, 'expert', split_axis=0, concat_axis=0, tiled=True)  95.2 us
    all_to_all x1, waiting for transfers between devices, on_device(): lax.all_to_all(jnp.stack([homeward.astype(jnp.bfloat16)] * lax.axis_size(...  87.8 us
    reduce_scatter x1, waiting for transfers between devices, on_device(): lax.psum_scatter(partial_terms.astype(jnp.bfloat16), 'etp', scatter_dimen...  66.2 us
    convert_element_type x2, local copies, waits for them, and re-layouts, on_device(): gathered = jnp.concatenate(lax.all_to_all(jnp.stack([homeward.astype(jnp....  19.6 us
    all_to_all x1, blocking collectives, on_device(): lax.all_to_all(summed.astype(jnp.bfloat16), 'expert', split_axis=0, conca...  16.7 us
    gather x2, local copies, waits for them, and re-layouts, on_device(): home_rows[(chosen * halves + half_index) * capacity + position]  15.9 us
    all_to_all x1, starting transfers between devices, on_device(): lax.all_to_all(jnp.stack([homeward.astype(jnp.bfloat16)] * lax.axis_size(...  11.7 us
    dot_general x1, matrix products, on_device(): term = jnp.dot(hidden, w_second, preferred_element_type=jnp.float32)  8.18 us
  transfers between devices with their start and end apart: 2, of which 2 were waited for; matrix products, arithmetic and copies ran while one was open for 0% of the time, Pallas kernels for 0%

profile of v1, /device:TPU:1, one launch (start us, length us, event | category | flops | bytes accessed | tf_op | source)
XLA Modules:
  0.0 377.9 jit_solution(17705078081651748386)
XLA Ops:
  6.5 0.9 copy.28
  7.7 0.7 add_multiply_fusion
  8.4 1.2 reduce-window.6
  10.8 1.9 broadcast_in_dim.7
  12.8 1.5 reshape.165
  14.3 4.2 %scatter_custom_fusion = bf16[320,3072]{1,0:T(8,128)(2,1)S(1)} fusion(s32[256]{0:T(256)S(1)} %bitcast.48, bf16[256,3072]{1,0:T(8,128)(2,1)} %reshape.165, bf16[]{:T(256)} %constant.5.clone.1), kind=kCustom, calls=%fused_computation.9 | custom fusion | bytes 1966592 | tf_op jit(solution)/shard_map/scatter | solution.py:25
  18.5 0.6 broadcast_in_dim.16
  19.1 95.2 %all_to_all.15 = bf16[8,80,3072]{2,1,0:T(8,128)(2,1)} all-to-all(bf16[8,80,3072]{2,1,0:T(8,128)(2,1)S(1)} %bitcast.40), channel_id=1, replica_groups=mesh['dp'=4,'expert'=8,'etp'=16] {'expert'}, dimensions={0} | all-to-all | bytes 7864320 | tf_op jit(solution)/shard_map/all_to_all | solution.py:30
  114.4 8.2 %convolution_convert_fusion = bf16[640,3072]{1,0:T(8,128)(2,1)} fusion(bf16[1,256,3072]{2,1,0:T(8,128)(2,1)S(1)} %copy-done, bf16[640,3072]{1,0:T(8,128)(2,1)} %bitcast.42, bf16[1,3072,256]{2,1,0:T(8,128)(2,1)S(1)} %copy-done.3), kind=kOutput, calls=%fused_computation.4 | convolution fusion | flops 2016051200 | bytes 11010048 | tf_op jit(solution)/shard_map/dot_general | solution.py:34
  122.5 6.2 %copy.32 = bf16[8,80,3072]{2,0,1:T(8,128)(2,1)} copy(bf16[8,80,3072]{2,1,0:T(8,128)(2,1)} %bitcast.43) | data formatting | bytes 7864320 | tf_op jit(solution)/shard_map/convert_element_type | solution.py:38
  128.7 66.2 %reduce-scatter.2.cloned.1.call-done = bf16[8,5,3072]{2,0,1:T(8,128)(2,1)} async-done(((bf16[8,80,3072]{2,0,1:T(8,128)(2,1)}), bf16[8,5,3072]{2,0,1:T(8,128)(2,1)}) %reduce-scatter.2.cloned.1.call-update) | async-done | bytes 245776 | tf_op jit(solution)/shard_map/reduce_scatter | solution.py:37
  194.9 1.1 copy.33
  196.0 16.7 %all_to_all.16 = bf16[8,5,3072]{2,1,0:T(8,128)(2,1)S(1)} all-to-all(bf16[8,5,3072]{2,1,0:T(8,128)(2,1)S(1)} %copy.33), channel_id=1, replica_groups=mesh['dp'=4,'expert'=8,'etp'=16] {'expert'}, dimensions={0} | all-to-all | bytes 491520 | tf_op jit(solution)/shard_map/all_to_all | solution.py:40
  212.9 2.4 stack.2
  215.3 11.7 %all-to-all-start.2 = ((bf16[16,8,5,3072]{3,1,2,0:T(8,128)(2,1)}), bf16[16,8,5,3072]{3,1,2,0:T(8,128)(2,1)}, u32[]{:S(2)}, u32[]{:S(2)}) async-start(bf16[16,8,5,3072]{3,1,2,0:T(8,128)(2,1)} %stack.2), calls=%async_computation.3 | async-start | bytes 7864320 | tf_op jit(solution)/shard_map/all_to_all | solution.py:44
  227.2 87.8 %all-to-all-done.2 = bf16[16,8,5,3072]{3,1,2,0:T(8,128)(2,1)} async-done(((bf16[16,8,5,3072]{3,1,2,0:T(8,128)(2,1)}), bf16[16,8,5,3072]{3,1,2,0:T(8,128)(2,1)}, u32[]{:S(2)}, u32[]{:S(2)}) %all-to-all-start.2) | async-done | bytes 3932192 | tf_op jit(solution)/shard_map/all_to_all | solution.py:44
  314.9 3.1 convert_bitcast_fusion
  318.1 9.4 %copy.35 = f32[8,16,5,3072]{3,2,1,0:T(8,128)} copy(f32[8,16,5,3072]{3,0,2,1:T(8,128)S(1)} %convert_bitcast_fusion) | data formatting | bytes 15728640 | tf_op jit(solution)/shard_map/convert_element_type | solution.py:48
  327.5 10.1 %reshape.144 = f32[640,3072]{1,0:T(8,128)} reshape(f32[8,16,5,3072]{3,2,1,0:T(8,128)} %copy.35) | data formatting | bytes 15728640 | tf_op jit(solution)/shard_map/convert_element_type | solution.py:48
  337.6 7.9 %gather_fusion.1 = f32[256,3072]{1,0:T(8,128)} fusion(f32[640,3072]{1,0:T(8,128)} %reshape.144, s32[1024]{0:T(1024)S(1)} %pad_clamp_fusion), kind=kCustom, calls=%fused_computation.1 | custom fusion | bytes 6292480 | tf_op jit(solution)/shard_map/gather | solution.py:52
  345.6 7.9 %gather_fusion = f32[256,3072]{1,0:T(8,128)} fusion(f32[640,3072]{1,0:T(8,128)} %reshape.144, s32[1024]{0:T(1024)S(1)} %pad_clamp_fusion.1), kind=kCustom, calls=%fused_computation | custom fusion | bytes 6292480 | tf_op jit(solution)/shard_map/gather | solution.py:52
  353.5 5.0 %add.100 = f32[256,3072]{1,0:T(8,128)} add(f32[256,3072]{1,0:T(8,128)} %gather_fusion, f32[256,3072]{1,0:T(8,128)} %gather_fusion.1) | non-fusion elementwise | flops 786432 | bytes 9437184 | tf_op jit(solution)/shard_map/add | solution.py:52
  358.6 5.2 %add.101 = f32[128,2,3072]{2,1,0:T(2,128)} reshape(f32[256,3072]{1,0:T(8,128)} %add.100) | data formatting | bytes 6291456 | tf_op jit(solution)/shard_map/add | solution.py:52
  363.7 7.3 %multiply_reduce_fusion = bf16[128,3072]{1,0:T(8,128)(2,1)} fusion(f32[128,2,3072]{2,1,0:T(2,128)} %add.101, f32[128,2]{1,0:T(8,128)S(1)} %copy.38), kind=kLoop, calls=%fused_computation.5 | loop fusion | flops 1179648 | bytes 3933184 | tf_op jit(solution)/shard_map/reduce_sum | solution.py:54
  (31 shorter events, 1.8 us)
Async XLA Ops:
  6.5 107.8 %copy-start = (bf16[1,256,3072]{2,1,0:T(8,128)(2,1)S(1)}, bf16[1,256,3072]{2,1,0:T(8,128)(2,1)}, u32[]{:S(2)}) copy-start(bf16[1,256,3072]{2,1,0:T(8,128)(2,1)} %param.9) | copy-start | bytes 4718596
  6.5 188.4 %reduce-scatter.2.cloned.1.call-start = ((), (), s32[]{:S(2)}) async-start(), calls=%async_computation.4 | async-start | bytes 4177920 | tf_op jit(solution)/shard_map/reduce_scatter | solution.py:37
  19.1 95.2 %copy-start.3 = (bf16[1,3072,256]{2,1,0:T(8,128)(2,1)S(1)}, bf16[1,3072,256]{2,1,0:T(8,128)(2,1)}, u32[]{:S(2)}) copy-start(bf16[1,3072,256]{2,1,0:T(8,128)(2,1)} %param.8) | copy-start | bytes 4718596
  215.3 11.7 %copy-start.2 = (f32[128,2]{0,1:T(2,128)S(1)}, f32[128,2]{0,1:T(2,128)}, u32[]{:S(2)}) copy-start(f32[128,2]{0,1:T(2,128)} %param.7) | copy-start | bytes 3076
  215.3 99.6 %all-to-all-start.2 = ((bf16[16,8,5,3072]{3,1,2,0:T(8,128)(2,1)}), bf16[16,8,5,3072]{3,1,2,0:T(8,128)(2,1)}, u32[]{:S(2)}, u32[]{:S(2)}) async-start(bf16[16,8,5,3072]{3,1,2,0:T(8,128)(2,1)} %stack.2), calls=%async_computation.3 | async-start | bytes 7864320 | tf_op jit(solution)/shard_map/all_to_all | solution.py:44
  358.5 12.5 %copy-start.1 = (bf16[1,256,3072]{2,1,0:T(8,128)(2,1)S(1)}, bf16[1,256,3072]{2,1,0:T(8,128)(2,1)}, u32[]{:S(2)}) copy-start(bf16[1,256,3072]{2,1,0:T(8,128)(2,1)} %param.9) | copy-start | bytes 4718596
Sparse Core Ops, SparseCore 0:
  128.9 66.0 reduce-scatter.1
